TPU v7x, 32 devices: a whole 2x2x4 slice. The times are simulated.
32 devices in a mesh: parts: 2 (over y), row: 4 (over z), col: 2 (over x), rhs: 2 (over core).
Axes of the slice: x: 2, y: 2, z: 4, core: 2. Of those that a mesh axis runs over, the one named last changes fastest.
Arguments:
- blocks: bfloat16 [8, 2, 96, 128, 128], P(('parts', 'row'), 'col'), parts along dimension 0, as said below
- block_rows: int32 [8, 2, 96], P(('parts', 'row'), 'col'), parts along dimension 0, may hold values from 0 to 127, as said below
- block_cols: int32 [8, 2, 96], P(('parts', 'row'), 'col'), parts along dimension 0, may hold values from 0 to 255, as said below
- counts: int32 [8, 2], P(('parts', 'row'), 'col'), parts along dimension 0, may hold values from 1 to 96, as said below
- diagonal: float32 [131072], P(('parts', 'row', 'col')), parts along dimension 0, may hold values from 1.2 to 4
- target: float32 [131072, 256], P(('parts', 'row', 'col'), 'rhs'), parts along dimension 0, may hold values from -6 to 6
Outputs:
- solution: float32 [131072, 256], P(('parts', 'row', 'col'), 'rhs'), parts along dimension 0
- residual: float32 [131072, 256], P(('parts', 'row', 'col'), 'rhs'), parts along dimension 0
There are 2 independent parts, one for each index of `parts`. A program takes and returns all parts, laid end to end along the dimension named above; each array names one. Nothing has to cross between parts.
Inputs may be any that keep to these rules, and one draw needn't show every extreme that they name: Each tile's used slots are its first counts slots; the busiest tile has exactly 96. `block_rows`: used slots of one tile name distinct blocks on or above the diagonal. `block_cols`: see block_rows. `blocks`: unused slots hold values that do not enter the operator; the operator is positive definite.
All inputs are finite; a program needn't handle non-finite values.
Results may differ from a plain program's by a relative error of at most 0.0045.
Values may be sent and summed in bfloat16 or wider, within the bound.
A program may use at most 128 MiB of HBM per device.

v0:
```python
import jax
import jax.numpy as jnp
from jax import lax
from jax.sharding import PartitionSpec as P

ITERS = 2


def one_hot_slots(indices, valid, extent):
    return ((indices[None, :] == jnp.arange(extent)[:, None]) & valid[None, :]).astype(jnp.float32)


def on_device(blocks, block_rows, block_cols, counts, diagonal, target):
    highest = lax.Precision.HIGHEST
    nrow = lax.axis_size("row")
    ncol = lax.axis_size("col")
    stored = blocks[0, 0]
    slots = stored.shape[0]
    width = stored.shape[1]
    local = target.shape[0]
    ncols = target.shape[1]
    quarter = local // width
    row_blocks = ncol * quarter
    col_blocks = nrow * quarter
    valid = jnp.arange(slots) < counts[0, 0]
    rows_hot = one_hot_slots(block_rows[0, 0], valid, row_blocks)
    cols_hot = one_hot_slots(block_cols[0, 0], valid, col_blocks)

    def squares(vector):
        return lax.psum(jnp.sum(vector * vector, axis=0), ("row", "col"))

    solution = jnp.zeros_like(target)
    residual = target
    direction = target
    norm_now = squares(residual)
    for step in range(ITERS):
        operate_field_low = direction.astype(jnp.bfloat16)
        direct_gathered = lax.all_gather(operate_field_low, "row", axis=0, tiled=True).reshape(
            col_blocks, width, ncols
        )
        prod = jnp.einsum(
            "kab,kbc->kac",
            stored,
            direct_gathered[block_cols[0, 0]],
            preferred_element_type=jnp.float32,
        )
        direct_partial_value = jnp.einsum("ik,kac->iac", rows_hot, prod, precision=highest)
        direct = lax.psum_scatter(
            direct_partial_value.reshape(row_blocks * width, ncols).astype(jnp.bfloat16),
            "col",
            scatter_dimension=0,
            tiled=True,
        ).astype(jnp.float32)
        gathered = lax.all_gather(operate_field_low, "col", axis=0, tiled=True).reshape(
            row_blocks, width, ncols
        )
        tprod = jnp.einsum(
            "kba,kbc->kac", stored, gathered[block_rows[0, 0]], preferred_element_type=jnp.float32
        )
        partial_value = jnp.einsum("jk,kac->jac", cols_hot, tprod, precision=highest)
        parcel = partial_value.astype(jnp.bfloat16).reshape(nrow, local, ncols)
        mirrored = jnp.sum(
            lax.all_to_all(parcel, "row", split_axis=0, concat_axis=0, tiled=True).astype(
                jnp.float32
            ),
            axis=0,
        )
        image = diagonal[:, None] * direction + direct + mirrored
        curve = lax.psum(jnp.sum(direction * image, axis=0), ("row", "col"))
        alpha = norm_now / curve
        solution = solution + alpha * direction
        residual = residual - alpha * image
        if step + 1 < ITERS:
            norm_next = squares(residual)
            direction = residual + norm_next / norm_now * direction
            norm_now = norm_next
    return (solution, residual)


def solution(mesh):
    return jax.shard_map(
        on_device,
        mesh=mesh,
        in_specs=(
            P(("parts", "row"), "col", None, None, None),
            P(("parts", "row"), "col", None),
            P(("parts", "row"), "col", None),
            P(("parts", "row"), "col"),
            P(("parts", "row", "col")),
            P(("parts", "row", "col"), "rhs"),
        ),
        out_specs=(P(("parts", "row", "col"), "rhs"), P(("parts", "row", "col"), "rhs")),
        check_vma=False,
    )
```

profile of v0, /device:TPU:0, one launch (start us, length us, event | category | flops | bytes accessed | tf_op | source)
XLA Modules:
  0.0 973.1 jit_solution(810773173325068209)
XLA Ops:
  12.6 58.2 %all-gather.7.cloned.1.call-done = bf16[16384,128]{1,0:T(8,128)(2,1)} async-done(((bf16[8192,128]{1,0:T(8,128)(2,1)}), bf16[16384,128]{1,0:T(8,128)(2,1)}) %all-gather.7.cloned.1.call-update) | async-done | bytes 4194320 | tf_op jit(solution)/shard_map/all_gather | solution.py:54
  75.6 6.2 fusion.10
  81.8 7.1 copy.13
  88.9 13.1 %convolution_convert_fusion.1 = bf16[256,128,128]{2,0,1:T(8,128)(2,1)} fusion(f32[96,128,128]{1,0,2:T(8,128)} %copy.13, s32[96]{0:T(128)S(1)} %bitcast.65, pred[96]{0:T(512)(128)(4,1)S(1)} %iota_compare_fusion.2), kind=kOutput, calls=%fused_computation.7 | convolution fusion | flops 4836081664 | bytes 14680544 | tf_op jit(solution)/shard_map/jk,kac->jac/dot_general | solution.py:60
  102.0 12.0 %copy.9 = bf16[256,128,128]{2,1,0:T(8,128)(2,1)} copy(bf16[256,128,128]{2,0,1:T(8,128)(2,1)} %convolution_convert_fusion.1) | data formatting | bytes 16777216 | tf_op jit(solution)/shard_map/convert_element_type | solution.py:61
  120.2 242.3 %all-gather.5.cloned.1.call-done = bf16[32768,128]{1,0:T(8,128)(2,1)} async-done(((bf16[8192,128]{1,0:T(8,128)(2,1)}), bf16[32768,128]{1,0:T(8,128)(2,1)}) %all-gather.5.cloned.1.call-update) | async-done | bytes 8388624 | tf_op jit(solution)/shard_map/all_gather | solution.py:38
  362.6 6.1 gather_fusion
  368.6 6.9 fusion.12
  375.5 6.6 copy.12
  382.2 7.1 fusion.14
  394.0 7.7 all-to-all-done
  401.7 7.0 convert_reduce_fusion.1
  408.7 37.9 %reduce-scatter.3.cloned.1.call-done = bf16[8192,128]{1,0:T(8,128)(2,1)} async-done(((bf16[16384,128]{1,0:T(8,128)(2,1)}), bf16[8192,128]{1,0:T(8,128)(2,1)}) %reduce-scatter.3.cloned.1.call-update) | async-done | bytes 2097168 | tf_op jit(solution)/shard_map/reduce_scatter | solution.py:48
  451.2 20.4 %all-reduce = (f32[128]{0:T(128)S(1)}, f32[128]{0:T(128)S(1)}) all-reduce(f32[128]{0:T(128)S(1)} %get-tuple-element.3, f32[128]{0:T(128)S(1)} %get-tuple-element.2), channel_id=1, replica_groups=mesh['parts'=2,'row'=4,'col'=2,'rhs'=2] {'row','col'}, use_global_device_ids=true, to_apply=%region_1.0 | all-reduce | flops 256 | bytes 2048 | tf_op jit(solution)/shard_map/psum | solution.py:30
  471.6 5.9 multiply_reduce_fusion.1
  477.6 17.1 %psum.30 = f32[128]{0:T(128)S(1)} all-reduce(f32[128]{0:T(128)S(1)} %get-tuple-element.6), channel_id=1, replica_groups=mesh['parts'=2,'row'=4,'col'=2,'rhs'=2] {'row','col'}, use_global_device_ids=true, to_apply=%region_7.0 | all-reduce | flops 128 | bytes 1024 | tf_op jit(solution)/shard_map/psum | solution.py:30
  500.6 55.0 %all-gather.11.cloned.1.call-done = bf16[16384,128]{1,0:T(8,128)(2,1)} async-done(((bf16[8192,128]{1,0:T(8,128)(2,1)}), bf16[16384,128]{1,0:T(8,128)(2,1)}) %all-gather.11.cloned.1.call-update) | async-done | bytes 4194320 | tf_op jit(solution)/shard_map/all_gather | solution.py:54
  560.5 6.1 fusion.6
  566.6 7.0 copy.15
  573.6 13.1 %convolution_convert_fusion = bf16[256,128,128]{2,0,1:T(8,128)(2,1)} fusion(f32[96,128,128]{1,0,2:T(8,128)} %copy.15, s32[96]{0:T(128)S(1)} %bitcast.66, pred[96]{0:T(512)(128)(4,1)S(1)} %iota_compare_fusion.2), kind=kOutput, calls=%fused_computation.6 | convolution fusion | flops 4836081664 | bytes 14680544 | tf_op jit(solution)/shard_map/jk,kac->jac/dot_general | solution.py:60
  586.7 12.1 %copy.11 = bf16[256,128,128]{2,1,0:T(8,128)(2,1)} copy(bf16[256,128,128]{2,0,1:T(8,128)(2,1)} %convolution_convert_fusion) | data formatting | bytes 16777216 | tf_op jit(solution)/shard_map/convert_element_type | solution.py:61
  604.5 242.3 %all-gather.9.cloned.1.call-done = bf16[32768,128]{1,0:T(8,128)(2,1)} async-done(((bf16[8192,128]{1,0:T(8,128)(2,1)}), bf16[32768,128]{1,0:T(8,128)(2,1)}) %all-gather.9.cloned.1.call-update) | async-done | bytes 8388624 | tf_op jit(solution)/shard_map/all_gather | solution.py:38
  846.8 6.1 gather_fusion.2
  852.9 6.9 fusion.8
  859.8 6.8 copy.14
  866.6 7.1 fusion.17
  878.3 7.6 all-to-all-done.1
  885.9 7.0 convert_reduce_fusion
  893.0 37.9 %reduce-scatter.5.cloned.1.call-done = bf16[8192,128]{1,0:T(8,128)(2,1)} async-done(((bf16[16384,128]{1,0:T(8,128)(2,1)}), bf16[8192,128]{1,0:T(8,128)(2,1)}) %reduce-scatter.5.cloned.1.call-update) | async-done | bytes 2097168 | tf_op jit(solution)/shard_map/reduce_scatter | solution.py:48
  930.9 5.9 multiply_reduce_fusion
  936.8 20.4 %psum.31 = f32[128]{0:T(128)S(1)} all-reduce(f32[128]{0:T(128)S(1)} %multiply_reduce_fusion), channel_id=1, replica_groups=mesh['parts'=2,'row'=4,'col'=2,'rhs'=2] {'row','col'}, use_global_device_ids=true, to_apply=%region_11.0 | all-reduce | flops 128 | bytes 1024 | tf_op jit(solution)/shard_map/psum | solution.py:69
  957.2 8.7 multiply_subtract_fusion
  (37 shorter events, 46.3 us)
Async XLA Ops:
  7.2 68.5 %copy-start = (bf16[1,1,96,128,128]{4,3,2,1,0:T(8,128)(2,1)S(1)}, bf16[1,1,96,128,128]{4,3,2,1,0:T(8,128)(2,1)}, u32[]{:S(2)}) copy-start(bf16[1,1,96,128,128]{4,3,2,1,0:T(8,128)(2,1)} %param.6) | copy-start | bytes 9437188
  7.2 5.4 copy-start.3
  7.2 63.5 %all-gather.7.cloned.1.call-start = ((), (), s32[]{:S(2)}) async-start(), calls=%async_computation.6 | async-start | bytes 6291456 | tf_op jit(solution)/shard_map/all_gather | solution.py:54
  11.1 351.4 %all-gather.5.cloned.1.call-start = ((), (), s32[]{:S(2)}) async-start(), calls=%async_computation.4 | async-start | bytes 10485760 | tf_op jit(solution)/shard_map/all_gather | solution.py:38
  81.8 7.1 copy-start.2
  114.1 287.7 %all-to-all-start = ((bf16[4,8192,128]{2,1,0:T(8,128)(2,1)}), bf16[4,8192,128]{2,1,0:T(8,128)(2,1)}, u32[]{:S(2)}, u32[]{:S(2)}) async-start(bf16[4,8192,128]{2,1,0:T(8,128)(2,1)} %bitcast.57), calls=%async_computation.1 | async-start | bytes 16777216 | tf_op jit(solution)/shard_map/all_to_all | solution.py:63
  119.7 326.8 %reduce-scatter.3.cloned.1.call-start = ((), (), s32[]{:S(2)}) async-start(), calls=%async_computation.5 | async-start | bytes 6291456 | tf_op jit(solution)/shard_map/reduce_scatter | solution.py:48
  394.0 52.6 %copy-start.1 = (f32[8192]{0:T(1024)S(1)}, f32[8192]{0:T(1024)}, u32[]{:S(2)}) copy-start(f32[8192]{0:T(1024)} %param.10) | copy-start | bytes 98308
  394.0 161.6 %all-gather.11.cloned.1.call-start = ((), (), s32[]{:S(2)}) async-start(), calls=%async_computation.9 | async-start | bytes 6291456 | tf_op jit(solution)/shard_map/all_gather | solution.py:54
  500.0 346.8 %all-gather.9.cloned.1.call-start = ((), (), s32[]{:S(2)}) async-start(), calls=%async_computation.7 | async-start | bytes 10485760 | tf_op jit(solution)/shard_map/all_gather | solution.py:38
  598.8 287.1 %all-to-all-start.1 = ((bf16[4,8192,128]{2,1,0:T(8,128)(2,1)}), bf16[4,8192,128]{2,1,0:T(8,128)(2,1)}, u32[]{:S(2)}, u32[]{:S(2)}) async-start(bf16[4,8192,128]{2,1,0:T(8,128)(2,1)} %bitcast.58), calls=%async_computation.3 | async-start | bytes 16777216 | tf_op jit(solution)/shard_map/all_to_all | solution.py:63
  604.5 326.4 %reduce-scatter.5.cloned.1.call-start = ((), (), s32[]{:S(2)}) async-start(), calls=%async_computation.8 | async-start | bytes 6291456 | tf_op jit(solution)/shard_map/reduce_scatter | solution.py:48
Sparse Core Ops, SparseCore 0:
  11.2 59.4 all-gather.6
  72.9 289.6 all-gather.4
  394.1 52.4 reduce-scatter.2
  500.1 55.4 all-gather.10
  557.1 289.6 all-gather.8
  878.4 52.4 reduce-scatter.4
where the time goes:
time: 976 us; the launch traced here: 973 us
  waiting for transfers between devices  690 us (71%)
  local copies, waits for them, and re-layouts  83 us (9%)
  matrix products  66.4 us (7%)
  blocking collectives  58 us (6%)
  other arithmetic  48.4 us (5%)
  between operations  15.1 us (2%)
  starting transfers between devices  12 us (1%)
    all_gather x2, waiting for transfers between devices, on_device(): lax.all_gather(operate_field_low, 'row', axis=0, tiled=True)  485 us
    all_gather x2, waiting for transfers between devices, on_device(): lax.all_gather(operate_field_low, 'col', axis=0, tiled=True)  113 us
    reduce_scatter x2, waiting for transfers between devices, on_device(): lax.psum_scatter(direct_partial_value.reshape(row_blocks * width, ncols)....  75.8 us
    psum x2, blocking collectives, squares(): return lax.psum(jnp.sum(vector * vector, axis=0), ('row', 'col'))  37.6 us
    dot_general x2, matrix products, on_device(): jnp.einsum('jk,kac->jac', cols_hot, tprod, precision=highest)  26.2 us
    convert_element_type x2, local copies, waits for them, and re-layouts, on_device(): parcel = partial_value.astype(jnp.bfloat16).reshape(nrow, local, ncols)  24.1 us
    psum x1, blocking collectives, on_device(): curve = lax.psum(jnp.sum(direction * image, axis=0), ('row', 'col'))  20.4 us
  transfers between devices with their start and end apart: 8, of which 8 were waited for; matrix products, arithmetic and copies ran while one was open for 17% of the time, Pallas kernels for 0%

commit v1 on v0

--- a/solution.py
+++ b/solution.py
@@ -66,7 +66,8 @@
             axis=0,
         )
         image = diagonal[:, None] * direction + direct + mirrored
-        curve = lax.psum(jnp.sum(direction * image, axis=0), ("row", "col"))
+        point = jnp.sum(direction * image, axis=0)
+        curve = lax.psum(lax.psum(point, "col"), "row")
         alpha = norm_now / curve
         solution = solution + alpha * direction
         residual = residual - alpha * image

time: 976 us -> 986 us (1.010)
  blocking collectives: 58 us -> 68.8 us
    psum x1 -> x4, blocking collectives: 20.4 us -> 29.9 us  [on_device(): curve = lax.psum(lax.psum(point, 'col'), 'row')]
where the time goes in v1:
time: 986 us; the launch traced here: 982 us
  waiting for transfers between devices  689 us (70%)
  local copies, waits for them, and re-layouts  83 us (8%)
  blocking collectives  68.8 us (7%)
  matrix products  66.4 us (7%)
  other arithmetic  48.4 us (5%)
  between operations  15.1 us (2%)
  starting transfers between devices  12 us (1%)
    all_gather x2, waiting for transfers between devices, on_device(): lax.all_gather(operate_field_low, 'row', axis=0, tiled=True)  485 us
    all_gather x2, waiting for transfers between devices, on_device(): lax.all_gather(operate_field_low, 'col', axis=0, tiled=True)  112 us
    reduce_scatter x2, waiting for transfers between devices, on_device(): lax.psum_scatter(direct_partial_value.reshape(row_blocks * width, ncols)....  75.8 us
    psum x2, blocking collectives, squares(): return lax.psum(jnp.sum(vector * vector, axis=0), ('row', 'col'))  39 us
    psum x4, blocking collectives, on_device(): curve = lax.psum(lax.psum(point, 'col'), 'row')  29.9 us
    dot_general x2, matrix products, on_device(): jnp.einsum('jk,kac->jac', cols_hot, tprod, precision=highest)  26.2 us
    convert_element_type x2, local copies, waits for them, and re-layouts, on_device(): parcel = partial_value.astype(jnp.bfloat16).reshape(nrow, local, ncols)  24.1 us
  transfers between devices with their start and end apart: 8, of which 8 were waited for; matrix products, arithmetic and copies ran while one was open for 17% of the time, Pallas kernels for 0%

profile of v1, /device:TPU:0, one launch (start us, length us, event | category | flops | bytes accessed | tf_op | source)
XLA Modules:
  0.0 982.5 jit_solution(16324997306976758205)
XLA Ops:
  12.6 58.2 %all-gather.7.cloned.1.call-done = bf16[16384,128]{1,0:T(8,128)(2,1)} async-done(((bf16[8192,128]{1,0:T(8,128)(2,1)}), bf16[16384,128]{1,0:T(8,128)(2,1)}) %all-gather.7.cloned.1.call-update) | async-done | bytes 4194320 | tf_op jit(solution)/shard_map/all_gather | solution.py:54
  75.6 6.2 fusion.10
  81.8 7.1 copy.13
  88.9 13.1 %convolution_convert_fusion.1 = bf16[256,128,128]{2,0,1:T(8,128)(2,1)} fusion(f32[96,128,128]{1,0,2:T(8,128)} %copy.13, s32[96]{0:T(128)S(1)} %bitcast.65, pred[96]{0:T(512)(128)(4,1)S(1)} %iota_compare_fusion.2), kind=kOutput, calls=%fused_computation.7 | convolution fusion | flops 4836081664 | bytes 14680544 | tf_op jit(solution)/shard_map/jk,kac->jac/dot_general | solution.py:60
  102.0 12.0 %copy.9 = bf16[256,128,128]{2,1,0:T(8,128)(2,1)} copy(bf16[256,128,128]{2,0,1:T(8,128)(2,1)} %convolution_convert_fusion.1) | data formatting | bytes 16777216 | tf_op jit(solution)/shard_map/convert_element_type | solution.py:61
  120.2 242.3 %all-gather.5.cloned.1.call-done = bf16[32768,128]{1,0:T(8,128)(2,1)} async-done(((bf16[8192,128]{1,0:T(8,128)(2,1)}), bf16[32768,128]{1,0:T(8,128)(2,1)}) %all-gather.5.cloned.1.call-update) | async-done | bytes 8388624 | tf_op jit(solution)/shard_map/all_gather | solution.py:38
  362.6 6.1 gather_fusion
  368.6 6.9 fusion.12
  375.5 6.6 copy.12
  382.2 7.1 fusion.14
  394.0 7.7 all-to-all-done
  401.7 7.0 convert_reduce_fusion.1
  408.7 37.9 %reduce-scatter.3.cloned.1.call-done = bf16[8192,128]{1,0:T(8,128)(2,1)} async-done(((bf16[16384,128]{1,0:T(8,128)(2,1)}), bf16[8192,128]{1,0:T(8,128)(2,1)}) %reduce-scatter.3.cloned.1.call-update) | async-done | bytes 2097168 | tf_op jit(solution)/shard_map/reduce_scatter | solution.py:48
  451.2 20.4 %psum.42 = f32[128]{0:T(128)S(1)} all-reduce(f32[128]{0:T(128)S(1)} %get-tuple-element.3), channel_id=1, replica_groups=mesh['parts'=2,'row'=4,'col'=2,'rhs'=2] {'row','col'}, use_global_device_ids=true, to_apply=%region_1.0 | all-reduce | flops 128 | bytes 1024 | tf_op jit(solution)/shard_map/psum | solution.py:30
  476.6 8.3 psum.44
  484.9 5.9 multiply_reduce_fusion.1
  490.8 18.5 %psum.45 = f32[128]{0:T(128)S(1)} all-reduce(f32[128]{0:T(128)S(1)} %get-tuple-element.4), channel_id=1, replica_groups=mesh['parts'=2,'row'=4,'col'=2,'rhs'=2] {'row','col'}, use_global_device_ids=true, to_apply=%region_8.0 | all-reduce | flops 128 | bytes 1024 | tf_op jit(solution)/shard_map/psum | solution.py:30
  515.3 53.6 %all-gather.11.cloned.1.call-done = bf16[16384,128]{1,0:T(8,128)(2,1)} async-done(((bf16[8192,128]{1,0:T(8,128)(2,1)}), bf16[16384,128]{1,0:T(8,128)(2,1)}) %all-gather.11.cloned.1.call-update) | async-done | bytes 4194320 | tf_op jit(solution)/shard_map/all_gather | solution.py:54
  573.8 6.1 fusion.6
  579.9 7.0 copy.15
  586.9 13.1 %convolution_convert_fusion = bf16[256,128,128]{2,0,1:T(8,128)(2,1)} fusion(f32[96,128,128]{1,0,2:T(8,128)} %copy.15, s32[96]{0:T(128)S(1)} %bitcast.66, pred[96]{0:T(512)(128)(4,1)S(1)} %iota_compare_fusion.2), kind=kOutput, calls=%fused_computation.6 | convolution fusion | flops 4836081664 | bytes 14680544 | tf_op jit(solution)/shard_map/jk,kac->jac/dot_general | solution.py:60
  600.0 12.1 %copy.11 = bf16[256,128,128]{2,1,0:T(8,128)(2,1)} copy(bf16[256,128,128]{2,0,1:T(8,128)(2,1)} %convolution_convert_fusion) | data formatting | bytes 16777216 | tf_op jit(solution)/shard_map/convert_element_type | solution.py:61
  617.8 242.3 %all-gather.9.cloned.1.call-done = bf16[32768,128]{1,0:T(8,128)(2,1)} async-done(((bf16[8192,128]{1,0:T(8,128)(2,1)}), bf16[32768,128]{1,0:T(8,128)(2,1)}) %all-gather.9.cloned.1.call-update) | async-done | bytes 8388624 | tf_op jit(solution)/shard_map/all_gather | solution.py:38
  860.0 6.1 gather_fusion.2
  866.1 6.9 fusion.8
  873.0 6.8 copy.14
  879.9 7.1 fusion.17
  891.6 7.6 all-to-all-done.1
  899.2 7.0 convert_reduce_fusion
  906.2 37.9 %reduce-scatter.5.cloned.1.call-done = bf16[8192,128]{1,0:T(8,128)(2,1)} async-done(((bf16[16384,128]{1,0:T(8,128)(2,1)}), bf16[8192,128]{1,0:T(8,128)(2,1)}) %reduce-scatter.5.cloned.1.call-update) | async-done | bytes 2097168 | tf_op jit(solution)/shard_map/reduce_scatter | solution.py:48
  955.0 11.7 %psum.47 = f32[128]{0:T(128)S(1)} all-reduce(f32[128]{0:T(128)S(1)} %psum.46), channel_id=1, replica_groups=mesh['parts'=2,'row'=4,'col'=2,'rhs'=2] {'row'}, use_global_device_ids=true, to_apply=%region_13.0 | all-reduce | flops 128 | bytes 1024 | tf_op jit(solution)/shard_map/psum | solution.py:70
  966.7 8.7 multiply_subtract_fusion
  (40 shorter events, 62.0 us)
Async XLA Ops:
  7.2 68.5 %copy-start = (bf16[1,1,96,128,128]{4,3,2,1,0:T(8,128)(2,1)S(1)}, bf16[1,1,96,128,128]{4,3,2,1,0:T(8,128)(2,1)}, u32[]{:S(2)}) copy-start(bf16[1,1,96,128,128]{4,3,2,1,0:T(8,128)(2,1)} %param.6) | copy-start | bytes 9437188
  7.2 5.4 copy-start.3
  7.2 63.5 %all-gather.7.cloned.1.call-start = ((), (), s32[]{:S(2)}) async-start(), calls=%async_computation.6 | async-start | bytes 6291456 | tf_op jit(solution)/shard_map/all_gather | solution.py:54
  11.1 351.4 %all-gather.5.cloned.1.call-start = ((), (), s32[]{:S(2)}) async-start(), calls=%async_computation.4 | async-start | bytes 10485760 | tf_op jit(solution)/shard_map/all_gather | solution.py:38
  81.8 7.1 copy-start.2
  114.1 287.7 %all-to-all-start = ((bf16[4,8192,128]{2,1,0:T(8,128)(2,1)}), bf16[4,8192,128]{2,1,0:T(8,128)(2,1)}, u32[]{:S(2)}, u32[]{:S(2)}) async-start(bf16[4,8192,128]{2,1,0:T(8,128)(2,1)} %bitcast.57), calls=%async_computation.1 | async-start | bytes 16777216 | tf_op jit(solution)/shard_map/all_to_all | solution.py:63
  119.7 326.8 %reduce-scatter.3.cloned.1.call-start = ((), (), s32[]{:S(2)}) async-start(), calls=%async_computation.5 | async-start | bytes 6291456 | tf_op jit(solution)/shard_map/reduce_scatter | solution.py:48
  394.0 52.6 %copy-start.1 = (f32[8192]{0:T(1024)S(1)}, f32[8192]{0:T(1024)}, u32[]{:S(2)}) copy-start(f32[8192]{0:T(1024)} %param.10) | copy-start | bytes 98308
  394.0 174.9 %all-gather.11.cloned.1.call-start = ((), (), s32[]{:S(2)}) async-start(), calls=%async_computation.9 | async-start | bytes 6291456 | tf_op jit(solution)/shard_map/all_gather | solution.py:54
  514.7 345.3 %all-gather.9.cloned.1.call-start = ((), (), s32[]{:S(2)}) async-start(), calls=%async_computation.7 | async-start | bytes 10485760 | tf_op jit(solution)/shard_map/all_gather | solution.py:38
  612.1 287.1 %all-to-all-start.1 = ((bf16[4,8192,128]{2,1,0:T(8,128)(2,1)}), bf16[4,8192,128]{2,1,0:T(8,128)(2,1)}, u32[]{:S(2)}, u32[]{:S(2)}) async-start(bf16[4,8192,128]{2,1,0:T(8,128)(2,1)} %bitcast.58), calls=%async_computation.3 | async-start | bytes 16777216 | tf_op jit(solution)/shard_map/all_to_all | solution.py:63
  617.7 326.4 %reduce-scatter.5.cloned.1.call-start = ((), (), s32[]{:S(2)}) async-start(), calls=%async_computation.8 | async-start | bytes 6291456 | tf_op jit(solution)/shard_map/reduce_scatter | solution.py:48
Sparse Core Ops, SparseCore 0:
  11.2 59.4 all-gather.6
  72.9 289.6 all-gather.4
  394.1 52.4 reduce-scatter.2
  514.8 53.9 all-gather.10
  570.4 289.6 all-gather.8
  891.7 52.4 reduce-scatter.4
